TPU v7x, 32 devices: a whole 2x2x4 slice. The times are simulated.
32 devices in a mesh: req: 16 (over z, x, core), tp: 2 (over y).
Axes of the slice: x: 2, y: 2, z: 4, core: 2. Of those that a mesh axis runs over, the one named last changes fastest.
Arguments:
- state: bfloat16 [256, 2048], P('req'), may hold values from -3 to 3
- norm_gain: float32 [2048], replicated, may hold values from 0.25 to 4
- w_qkv: bfloat16 [2048, 2, 512], P(None, 'tp'), may hold values from -0.125 to 0.125
- w_out: bfloat16 [2, 256, 2048], P('tp'), may hold values from -0.25 to 0.25
- kv_cache: bfloat16 [2944, 2, 16, 256], P('req', 'tp')
- lengths: int32 [256], P('req'), may hold values from 32 to 1024, as said below
- page_table: int32 [256, 64], P('req'), may hold values from 0 to 183, as said below
- dest_slot: int32 [256], P('req'), may hold values from 0 to 255, as said below
Outputs:
- new_state: bfloat16 [256, 2048], P('req')
Inputs may be any that keep to these rules, and one draw needn't show every extreme that they name: `lengths`: each device of req holds at most one request with more than 128 cached tokens; all others have 32 to 128; in every draw some request has exactly 1024. `page_table`: entry j of row r, for j below ceil(lengths[r] / 16), is the page (numbered within the home device r // 16) holding tokens j * 16 to (j + 1) * 16 - 1 of request r; no page serves two such entries; the entries after those are 183. dest_slot is a permutation. The request in slot k of device i of req (index i * 16 + k) goes to slot k of device (i + o_k) mod (16), with offsets o_k the same for all devices; at most 2 requests of one device go to one device, and exactly 2 do for some pairs.
All inputs are finite; a program needn't handle non-finite values.
Results may differ from a plain program's by a relative error of at most 0.01.
Values may be sent and summed in bfloat16 or wider, within the bound.
A program may use at most 64 MiB of HBM per device.

v0:
```python
import jax
import jax.numpy as jnp
from jax import lax
from jax.sharding import PartitionSpec as P


def normalize(values, scale_gain):
    wide = values.astype(jnp.float32)
    factor = lax.rsqrt(jnp.mean(wide * wide, axis=-1, keepdims=True) + 1e-05)
    return (wide * factor * scale_gain).astype(jnp.bfloat16)


def rotate(values, positions):
    half_size = values.shape[-1] // 2
    freqs = jnp.exp(
        -jnp.log(1000000.0) * 2.0 * jnp.arange(half_size, dtype=jnp.float32) / (2 * half_size)
    )
    angles = positions.astype(jnp.float32)[:, None, None] * freqs
    cosine = jnp.cos(angles)
    sine = jnp.sin(angles)
    first = values[..., :half_size]
    second = values[..., half_size:]
    return jnp.concatenate(
        [first * cosine - second * sine, second * cosine + first * sine], axis=-1
    )


def attend(query, new_key, new_value, page_pool, lengths, page_table):
    row_count = query.shape[0]
    group_size = query.shape[1]
    head_size = query.shape[2]
    page_count = page_pool.shape[0]
    page_size = page_pool.shape[1]
    table_width = page_table.shape[1]
    scale = 1.0 / jnp.sqrt(jnp.float32(head_size))
    used_pages = (lengths + page_size - 1) // page_size
    valid = jnp.arange(table_width, dtype=jnp.int32)[None, :] < used_pages[:, None]
    matches = (
        page_table[:, :, None] == jnp.arange(page_count, dtype=jnp.int32)[None, None, :]
    ) & valid[:, :, None]
    owner_int = jnp.sum(matches.astype(jnp.int32), axis=1)
    owner = owner_int.astype(jnp.float32)
    offsets = (jnp.arange(table_width, dtype=jnp.int32) * page_size)[None, :, None]
    page_base = jnp.sum(matches.astype(jnp.int32) * offsets, axis=(0, 1))
    page_limit = jnp.sum(owner_int * lengths[:, None], axis=0)
    live = (
        page_base[:, None] + jnp.arange(page_size, dtype=jnp.int32)[None, :] < page_limit[:, None]
    )
    page_query = jnp.dot(
        owner.T.astype(jnp.bfloat16),
        query.reshape(row_count, group_size * head_size),
        preferred_element_type=jnp.float32,
    )
    page_query = page_query.astype(jnp.bfloat16).reshape(page_count, group_size, head_size)
    scores = (
        jnp.einsum(
            "pjc,ptc->pjt",
            page_query,
            page_pool[:, :, :head_size],
            preferred_element_type=jnp.float32,
        )
        * scale
    )
    scores = jnp.where(live[:, None, :], scores, -jnp.inf)
    score_new = jnp.einsum("rjc,rc->rj", query, new_key, preferred_element_type=jnp.float32) * scale
    page_top = jnp.max(scores, axis=-1)
    row_top = jnp.max(jnp.where(owner_int[:, :, None] > 0, page_top[None, :, :], -jnp.inf), axis=1)
    row_top = jnp.maximum(row_top, score_new)
    spread_top = jnp.dot(owner.T, row_top, precision=lax.Precision.HIGHEST)
    weights = jnp.exp(scores - spread_top[:, :, None])
    weight_new = jnp.exp(score_new - row_top)
    total = jnp.dot(owner, jnp.sum(weights, axis=-1), precision=lax.Precision.HIGHEST) + weight_new
    page_sums = jnp.einsum(
        "pjt,ptc->pjc",
        weights.astype(jnp.bfloat16),
        page_pool[:, :, head_size:],
        preferred_element_type=jnp.float32,
    )
    numer = jnp.dot(
        owner,
        page_sums.reshape(page_count, group_size * head_size),
        precision=lax.Precision.HIGHEST,
    )
    numer = numer.reshape(row_count, group_size, head_size)
    numer = (
        numer
        + weight_new.astype(jnp.bfloat16).astype(jnp.float32)[:, :, None]
        * new_value.astype(jnp.float32)[:, None, :]
    )
    return (
        (numer / total[:, :, None]).astype(jnp.bfloat16).reshape(row_count, group_size * head_size)
    )


def relocate(mixed, dest_slot):
    row_count = mixed.shape[0]
    device_count = lax.axis_size("req")
    own_index = lax.axis_index("req")
    target_device = dest_slot // row_count
    shift_amount = (target_device - own_index) % device_count
    collected = lax.all_gather(mixed, "req", axis=0, tiled=True)
    source_device = (own_index - shift_amount) % device_count
    source_rows = source_device * row_count + jnp.arange(row_count, dtype=jnp.int32)
    return jnp.take(collected, source_rows, axis=0)


def local(state, norm_gain, w_qkv, w_out, kv_cache, lengths, page_table, dest_slot):
    row_count = state.shape[0]
    width = state.shape[1]
    head_size = kv_cache.shape[3] // 2
    group_size = w_out.shape[1] // head_size
    normed = normalize(state, norm_gain)
    proj = jnp.dot(normed, w_qkv.reshape(width, w_qkv.shape[2]), preferred_element_type=jnp.float32)
    query = rotate(
        proj[:, : group_size * head_size].reshape(row_count, group_size, head_size), lengths
    ).astype(jnp.bfloat16)
    new_key = rotate(proj[:, None, group_size * head_size : (group_size + 1) * head_size], lengths)[
        :, 0
    ].astype(jnp.bfloat16)
    new_value = proj[:, (group_size + 1) * head_size :].astype(jnp.bfloat16)
    attn = attend(query, new_key, new_value, kv_cache[:, 0], lengths, page_table)
    partial_out = jnp.dot(attn, w_out[0], preferred_element_type=jnp.float32)
    summed = lax.psum(partial_out, "tp")
    mixed = (state.astype(jnp.float32) + summed).astype(jnp.bfloat16)
    return relocate(mixed, dest_slot)


def solution(mesh):
    placed = (
        P("req", None),
        P(),
        P(None, "tp", None),
        P("tp", None, None),
        P("req", "tp", None, None),
        P("req"),
        P("req", None),
        P("req"),
    )
    return jax.shard_map(
        local, mesh=mesh, in_specs=placed, out_specs=P("req", None), check_vma=False
    )
```

profile of v0, /device:TPU:0, one launch (start us, length us, event | category | flops | bytes accessed | tf_op | source)
XLA Modules:
  0.0 92.7 jit_solution(18286603399373292580)
XLA Ops:
  6.6 0.8 fusion.54
  7.5 1.2 %select_reduce_fusion = (s32[184]{0:T(256)S(1)}, s32[16,184]{1,0:T(8,128)S(1)}) fusion(s32[64]{0:T(128)S(1)} %iota_multiply_fusion, s32[16,64]{1,0:T(8,128)} %param.14, pred[16,64]{1,0:T(8,128)(4,1)S(1)} %iota_compare_fusion.1), kind=kLoop, calls=%fused_computation.13 | loop fusion | flops 1127368 | bytes 17888 | tf_op jit(solution)/shard_map/reduce_sum | solution.py:44
  8.7 0.7 multiply_reduce_fusion
  9.4 1.0 %fusion.14 = f32[16]{0:T(128)S(1)} fusion(bf16[16,2048]{1,0:T(8,128)(2,1)} %param.8), kind=kLoop, calls=%fused_computation.27 | loop fusion | flops 98288 | bytes 65600 | tf_op jit(solution)/shard_map/reduce_sum | solution.py:9
  10.4 1.3 %fusion = f32[16,512]{1,0:T(8,128)S(1)} fusion(bf16[2048,1,512]{2,0,1:T(8,128)(2,1)S(1)} %copy-done, bf16[16,2048]{1,0:T(8,128)(2,1)} %param.8, f32[2048]{0:T(1024)} %param.9, f32[16]{0:T(128)S(1)} %add_rsqrt_fusion), kind=kOutput, calls=%fused_computation.1 | convolution fusion | flops 33685504 | bytes 2203712 | tf_op jit(solution)/shard_map/dot_general | solution.py:113
  11.7 0.1 multiply_cosine_fusion.1
  11.8 0.1 multiply_subtract_fusion
  12.0 0.2 convolution_convert_fusion
  12.3 0.1 add_compare_fusion
  12.4 1.7 %fusion.55 = (f32[184,2]{1,0:T(8,128)S(1)}, f32[184,2,16]{2,1,0:T(2,128)S(1)}) fusion(bf16[184,2,128]{2,1,0:T(2,128)(2,1)S(1)} %reshape.207, bf16[184,16,256]{2,1,0:T(8,128)(2,1)} %bitcast.55, pred[184,16]{1,0:T(8,128)(4,1)S(1)} %add_compare_fusion), kind=kOutput, calls=%fused_computation.105 | convolution fusion | flops 1524624 | bytes 875840 | tf_op jit(solution)/shard_map/pjc,ptc->pjt/dot_general | solution.py:56
  14.2 0.1 fusion.35
  14.4 0.1 fusion.42
  14.6 0.1 select_reduce_fusion.1
  14.7 0.4 fusion.28
  15.1 1.6 %fusion.9 = f32[184,2,128]{2,1,0:T(2,128)S(1)} fusion(bf16[184,16,256]{2,1,0:T(8,128)(2,1)} %bitcast.56, f32[184,2,16]{2,1,0:T(2,128)S(1)} %get-tuple-element.18, f32[184,2]{1,0:T(8,128)S(1)} %fusion.28), kind=kOutput, calls=%fused_computation.17 | convolution fusion | flops 1519104 | bytes 967104 | tf_op jit(solution)/shard_map/pjt,ptc->pjc/dot_general | solution.py:73
  16.7 0.5 fusion.18
  17.2 0.3 convolution_add_fusion.1
  17.5 0.2 fusion.5
  17.8 0.9 fusion.6
  18.7 24.2 %all-reduce.2.cloned.1.call-done = f32[16,2048]{1,0:T(8,128)} async-done(((f32[16,2048]{1,0:T(8,128)}), f32[16,2048]{1,0:T(8,128)}) %all-reduce.2.cloned.1.call-update) | async-done | bytes 131088 | tf_op jit(solution)/shard_map/psum | solution.py:123
  43.0 1.5 %fusion.17 = bf16[16,2048]{1,0:T(8,128)(2,1)} fusion(f32[16,2048]{1,0:T(8,128)} %all-reduce.2.cloned.1.call-done, bf16[16,2048]{1,0:T(8,128)(2,1)S(1)} %copy-done.2), kind=kLoop, calls=%fused_computation.30 | loop fusion | flops 98304 | bytes 262144 | tf_op jit(solution)/shard_map/convert_element_type | solution.py:124
  44.6 38.5 %all-gather.2.cloned.1.call-done = bf16[256,2048]{1,0:T(8,128)(2,1)} async-done(((bf16[16,2048]{1,0:T(8,128)(2,1)}), bf16[256,2048]{1,0:T(8,128)(2,1)}) %all-gather.2.cloned.1.call-update) | async-done | bytes 1048592 | tf_op jit(solution)/shard_map/all_gather | solution.py:101
  83.1 2.0 %gather_fusion = bf16[16,2048]{1,0:T(8,128)(2,1)S(1)} fusion(bf16[256,2048]{1,0:T(8,128)(2,1)} %all-gather.2.cloned.1.call-done, s32[1024]{0:T(1024)S(1)} %pad_clamp_fusion), kind=kCustom, calls=%fused_computation | custom fusion | bytes 131136 | tf_op jit(solution)/shard_map/jit(_take)/gather | solution.py:104
  85.1 0.7 broadcast_select_fusion
  (29 shorter events, 0.6 us)
Async XLA Ops:
  6.5 3.9 %copy-start = (bf16[2048,1,512]{2,0,1:T(8,128)(2,1)S(1)}, bf16[2048,1,512]{2,0,1:T(8,128)(2,1)}, u32[]{:S(2)}) copy-start(bf16[2048,1,512]{2,0,1:T(8,128)(2,1)} %param.10) | copy-start | bytes 6291460
  6.5 36.4 %all-reduce.2.cloned.1.call-start = ((), (), s32[]{:S(2)}) async-start(), calls=%async_computation | async-start | bytes 262144 | tf_op jit(solution)/shard_map/psum | solution.py:123
  14.1 3.7 %copy-start.1 = (bf16[1,256,2048]{2,1,0:T(8,128)(2,1)S(1)}, bf16[1,256,2048]{2,1,0:T(8,128)(2,1)}, u32[]{:S(2)}) copy-start(bf16[1,256,2048]{2,1,0:T(8,128)(2,1)} %param.11) | copy-start | bytes 3145732
  15.1 27.9 %copy-start.2 = (bf16[16,2048]{1,0:T(8,128)(2,1)S(1)}, bf16[16,2048]{1,0:T(8,128)(2,1)}, u32[]{:S(2)}) copy-start(bf16[16,2048]{1,0:T(8,128)(2,1)} %param.8) | copy-start | bytes 196612
  16.7 27.9 %copy-start.3 = (s32[16]{0:T(128)S(1)}, s32[16]{0:T(128)}, u32[]{:S(2)}) copy-start(s32[16]{0:T(128)} %param.15) | copy-start | bytes 196
  18.7 64.4 %all-gather.2.cloned.1.call-start = ((), (), s32[]{:S(2)}) async-start(), calls=%async_computation.1 | async-start | bytes 1114112 | tf_op jit(solution)/shard_map/all_gather | solution.py:101
Sparse Core Ops, SparseCore 0:
  18.8 24.1 all-reduce.1
  45.1 37.9 all-gather.1
where the time goes:
time: 93.1 us; the launch traced here: 92.7 us
  waiting for transfers between devices  62.8 us (67%)
  between operations  13.6 us (15%)
  other arithmetic  7.4 us (8%)
  matrix products  6.65 us (7%)
  local copies, waits for them, and re-layouts  2.24 us (2%)
    all_gather x1, waiting for transfers between devices, relocate(): collected = lax.all_gather(mixed, 'req', axis=0, tiled=True)  38.5 us
    psum x1, waiting for transfers between devices, local(): summed = lax.psum(partial_out, 'tp')  24.2 us
    gather x1, local copies, waits for them, and re-layouts, relocate(): return jnp.take(collected, source_rows, axis=0)  2.02 us
  transfers between devices with their start and end apart: 2, of which 2 were waited for; matrix products, arithmetic and copies ran while one was open for 0% of the time, Pallas kernels for 0%

commit v1 on v0

v1 whole, which is shorter than its diff:
```python
import functools
import math

import jax
import jax.numpy as jnp
from jax import lax
from jax.experimental import pallas as pl
from jax.experimental.pallas import tpu as pltpu
from jax.sharding import PartitionSpec as P

MESH = pl.DeviceIdType.MESH
LANES = 128
F32 = jnp.float32
BF16 = jnp.bfloat16


def iota(shape, axis):
    return lax.broadcasted_iota(jnp.int32, shape, axis)


def to_column(row):
    size = row.shape[1]
    eye = iota((size, size), 0) == iota((size, size), 1)
    return jnp.sum(jnp.where(eye, jnp.broadcast_to(row, (size, size)), 0.0), axis=1, keepdims=True)


def kernel(
    n,
    tp,
    page,
    state_ref,
    gain_ref,
    wqkv_hbm,
    wout_hbm,
    pool_hbm,
    len_ref,
    table_ref,
    dest_ref,
    out_ref,
    wqkv,
    wout,
    pool,
    parts,
    arrived,
    outgoing,
    incoming,
    gathered,
    load_sem,
    part_send,
    part_recv,
    move_send,
    move_recv,
    gather_send,
    gather_recv,
):
    rows, width = state_ref.shape
    group = wout.shape[0] // LANES
    chunk = width // tp
    blocks = chunk // LANES
    tokens = pool.shape[0]
    page_count = tokens // page
    me = lax.axis_index("req")
    my_part = lax.axis_index("tp")

    steps = 4
    depth = width // steps
    loads = []
    for step in range(steps):
        span = pl.ds(step * depth, depth)
        loads.append(pltpu.make_async_copy(wqkv_hbm.at[span], wqkv.at[span], load_sem.at[step]))
    load_pool = pltpu.make_async_copy(pool_hbm, pool, load_sem.at[steps])
    load_wout = pltpu.make_async_copy(wout_hbm, wout, load_sem.at[steps + 1])
    for load in loads:
        load.start()
    load_pool.start()
    load_wout.start()

    barrier = pltpu.get_barrier_semaphore()

    def greet(shift, carry):
        pl.semaphore_signal(
            barrier,
            inc=1,
            device_id={"req": lax.rem(me + shift, n), "tp": my_part},
            device_id_type=MESH,
        )
        return carry

    lax.fori_loop(1, n, greet, 0)
    for shift in range(1, tp):
        pl.semaphore_signal(
            barrier,
            inc=1,
            device_id={"req": me, "tp": lax.rem(my_part + shift, tp)},
            device_id_type=MESH,
        )

    wide = state_ref[...].astype(F32)
    factor = lax.rsqrt(jnp.mean(wide * wide, axis=-1, keepdims=True) + 1e-05)
    normed = (wide * factor * gain_ref[...]).astype(BF16)

    length = to_column(len_ref[...].astype(F32))
    lane = iota((rows, LANES), 1)
    half = LANES // 2
    index = lax.rem(lane, half).astype(F32)
    freqs = jnp.exp(-math.log(1000000.0) * 2.0 * index / LANES)
    angles = length * freqs
    cosine = jnp.cos(angles)
    sine = jnp.where(lane < half, -jnp.sin(angles), jnp.sin(angles))

    used = jnp.floor((length + (page - 1)) / page).astype(jnp.int32)
    table = table_ref[...]
    table = jnp.where(iota(table.shape, 1) < used, table, -1)
    padded = pl.cdiv(page_count, LANES) * LANES
    page_id = iota((rows, padded), 1)
    live_count = jnp.zeros((rows, padded), F32)
    for entry in range(table.shape[1]):
        left = length - float(entry * page)
        live_count = jnp.where(page_id == table[:, entry : entry + 1], left, live_count)
    live_count = jnp.clip(live_count, 0.0, float(page))
    per_block = LANES // page
    shifted = []
    for block in range(tokens // LANES):
        first = block * per_block
        base = first // LANES * LANES
        piece = live_count[:, base : base + LANES]
        if first != base:
            piece = pltpu.roll(piece, LANES - (first - base), 1)
        shifted.append(piece)
    spread = (iota((LANES, LANES), 0) == iota((LANES, LANES), 1) // page).astype(BF16)
    live_tokens = jnp.dot(
        jnp.concatenate(shifted, axis=0).astype(BF16), spread, preferred_element_type=F32
    )

    shift_bits = rows.bit_length() - 1
    target_row = lax.shift_right_logical(dest_ref[...], shift_bits).astype(F32)
    target = to_column(target_row)
    same = jnp.broadcast_to(target, (rows, rows)) == jnp.broadcast_to(target_row, (rows, rows))
    earlier = iota((rows, rows), 1) < iota((rows, rows), 0)
    rank = jnp.sum(jnp.where(same & earlier, 1.0, 0.0), axis=1, keepdims=True)
    source = (2 * me).astype(F32) - target
    source = jnp.where(source < 0, source + n, source)
    source = jnp.where(source >= n, source - n, source)
    key_out = (target * 2 + rank).astype(jnp.int32)
    key_in = (source * 2 + rank).astype(jnp.int32)
    flat = rows * blocks
    total_rows = n * 2 * blocks
    picked = iota((rows, flat), 0) == lax.rem(iota((rows, flat), 1), rows)
    key_row = jnp.sum(jnp.where(picked, key_out, 0).astype(F32), axis=0, keepdims=True).astype(
        jnp.int32
    )
    row_id = iota((total_rows, flat), 0)
    col_id = iota((total_rows, flat), 1)
    pack = (
        (row_id // blocks == key_row) & (lax.rem(row_id, blocks) == col_id // rows)
    ).astype(BF16)
    key_col = jnp.concatenate([key_in] * blocks, axis=0)
    row_id = iota((flat, total_rows), 0)
    col_id = iota((flat, total_rows), 1)
    unpack = (
        (col_id // blocks == key_col) & (lax.rem(col_id, blocks) == row_id // rows)
    ).astype(BF16)

    proj = None
    for step in range(steps):
        loads[step].wait()
        span = slice(step * depth, (step + 1) * depth)
        term = jnp.dot(normed[:, span], wqkv[span, :], preferred_element_type=F32)
        proj = term if proj is None else proj + term

    def rotated(values):
        return (values * cosine + pltpu.roll(values, half, 1) * sine).astype(BF16)

    heads = [rotated(proj[:, g * LANES : (g + 1) * LANES]) for g in range(group)]
    new_key = rotated(proj[:, group * LANES : (group + 1) * LANES])
    new_value = proj[:, (group + 1) * LANES :].astype(BF16)
    query = jnp.concatenate(heads, axis=0)

    scale = 1.0 / math.sqrt(LANES)
    load_pool.wait()
    scores = lax.dot_general(
        query, pool[:, :LANES], (((1,), (1,)), ((), ())), preferred_element_type=F32
    )
    offset = lax.rem(lane, page).astype(F32)
    masked = []
    for block in range(tokens // LANES):
        live = live_tokens[block * rows : (block + 1) * rows] > offset
        piece = scores[:, block * LANES : (block + 1) * LANES] * scale
        masked.append(
            jnp.concatenate(
                [
                    jnp.where(live, piece[g * rows : (g + 1) * rows], -jnp.inf)
                    for g in range(group)
                ],
                axis=0,
            )
        )
    scores = jnp.concatenate(masked, axis=1)
    keys = jnp.concatenate([new_key] * group, axis=0).astype(F32)
    values = jnp.concatenate([new_value] * group, axis=0).astype(F32)
    score_new = jnp.sum(query.astype(F32) * keys, axis=1, keepdims=True) * scale
    top = jnp.maximum(jnp.max(scores, axis=1, keepdims=True), score_new)
    weights = jnp.exp(scores - top)
    weight_new = jnp.exp(score_new - top)
    total = jnp.sum(weights, axis=1, keepdims=True) + weight_new
    numer = jnp.dot(weights.astype(BF16), pool[:, LANES:], preferred_element_type=F32)
    numer = numer + weight_new.astype(BF16).astype(F32) * values
    attn = (numer / total).astype(BF16)
    attn = jnp.concatenate([attn[g * rows : (g + 1) * rows] for g in range(group)], axis=1)

    load_wout.wait()
    pl.semaphore_wait(barrier, n - 1 + tp - 1)

    def columns(part):
        return pl.ds(pl.multiple_of(part * chunk, chunk), chunk)

    def part_copy(slot, landing, peer):
        return pltpu.make_async_remote_copy(
            src_ref=parts.at[slot],
            dst_ref=arrived.at[landing],
            send_sem=part_send.at[slot],
            recv_sem=part_recv.at[landing],
            device_id={"req": me, "tp": peer},
            device_id_type=MESH,
        )

    for shift in range(1, tp):
        peer = lax.rem(my_part + shift, tp)
        parts[peer] = jnp.dot(attn, wout[:, columns(peer)], preferred_element_type=F32)
        part_copy(peer, my_part, peer).start()
    summed = jnp.dot(attn, wout[:, columns(my_part)], preferred_element_type=F32)
    for shift in range(1, tp):
        peer = lax.rem(my_part + shift, tp)
        part_copy(peer, peer, peer).wait_recv()
        summed = summed + arrived[peer]
    mixed = (state_ref[:, columns(my_part)].astype(F32) + summed).astype(BF16)

    stacked = jnp.concatenate(
        [mixed[:, b * LANES : (b + 1) * LANES] for b in range(blocks)], axis=0
    )
    packed = jnp.dot(pack, stacked, preferred_element_type=F32)
    outgoing[...] = packed.reshape(n, 2 * blocks, LANES).astype(BF16)

    def send(shift, carry):
        peer = lax.rem(me + shift, n)
        pltpu.make_async_remote_copy(
            src_ref=outgoing.at[peer],
            dst_ref=incoming.at[me],
            send_sem=move_send,
            recv_sem=move_recv,
            device_id={"req": peer, "tp": my_part},
            device_id_type=MESH,
        ).start()
        return carry

    lax.fori_loop(1, n, send, 0)
    incoming[me] = outgoing[me]
    all_but_one = pl.ds(0, n - 1)
    pltpu.make_async_copy(
        outgoing.at[all_but_one], incoming.at[all_but_one], move_recv
    ).wait()
    received = incoming[...].astype(F32).reshape(total_rows, LANES).astype(BF16)
    moved = jnp.dot(unpack, received, preferred_element_type=F32).astype(BF16)
    share = jnp.concatenate(
        [moved[b * rows : (b + 1) * rows] for b in range(blocks)], axis=1
    )

    gathered[my_part] = share

    def gather_copy(landing, peer, slot):
        return pltpu.make_async_remote_copy(
            src_ref=gathered.at[landing],
            dst_ref=gathered.at[landing],
            send_sem=gather_send.at[slot],
            recv_sem=gather_recv.at[landing],
            device_id={"req": me, "tp": peer},
            device_id_type=MESH,
        )

    for shift in range(1, tp):
        peer = lax.rem(my_part + shift, tp)
        gather_copy(my_part, peer, shift).start()
    out_ref[:, columns(my_part)] = share
    for shift in range(1, tp):
        peer = lax.rem(my_part + shift, tp)
        gather_copy(peer, peer, shift).wait_recv()
        out_ref[:, columns(peer)] = gathered[peer]
    for shift in range(1, tp):
        peer = lax.rem(my_part + shift, tp)
        gather_copy(my_part, peer, shift).wait_send()
        part_copy(peer, my_part, peer).wait_send()
    pltpu.make_async_copy(
        outgoing.at[all_but_one], incoming.at[all_but_one], move_send
    ).wait()


def local(n, tp, state, norm_gain, w_qkv, w_out, kv_cache, lengths, page_table, dest_slot):
    rows, width = state.shape
    page_count, _, page, entry = kv_cache.shape
    tokens = page_count * page
    chunk = width // tp
    blocks = chunk // LANES
    vmem = pl.BlockSpec(memory_space=pltpu.VMEM)
    hbm = pl.BlockSpec(memory_space=pltpu.HBM)
    return pl.pallas_call(
        functools.partial(kernel, n, tp, page),
        out_shape=jax.ShapeDtypeStruct((rows, width), BF16),
        in_specs=[vmem, vmem, hbm, hbm, hbm, vmem, vmem, vmem],
        out_specs=vmem,
        scratch_shapes=[
            pltpu.VMEM((width, w_qkv.shape[2]), BF16),
            pltpu.VMEM((w_out.shape[1], width), BF16),
            pltpu.VMEM((tokens, entry), BF16),
            pltpu.VMEM((tp, rows, chunk), F32),
            pltpu.VMEM((tp, rows, chunk), F32),
            pltpu.VMEM((n, 2 * blocks, LANES), BF16),
            pltpu.VMEM((n, 2 * blocks, LANES), BF16),
            pltpu.VMEM((tp, rows, chunk), BF16),
            pltpu.SemaphoreType.DMA((6,)),
            pltpu.SemaphoreType.DMA((tp,)),
            pltpu.SemaphoreType.DMA((tp,)),
            pltpu.SemaphoreType.DMA,
            pltpu.SemaphoreType.DMA,
            pltpu.SemaphoreType.DMA((tp,)),
            pltpu.SemaphoreType.DMA((tp,)),
        ],
        compiler_params=pltpu.CompilerParams(
            collective_id=0, has_side_effects=True, vmem_limit_bytes=32 * 1024 * 1024
        ),
    )(
        state,
        norm_gain.reshape(1, width),
        w_qkv.reshape(width, w_qkv.shape[2]),
        w_out[0],
        kv_cache.reshape(tokens, entry),
        lengths.reshape(1, rows),
        page_table,
        dest_slot.reshape(1, rows),
    )


def solution(mesh):
    placed = (
        P("req", None),
        P(),
        P(None, "tp", None),
        P("tp", None, None),
        P("req", "tp", None, None),
        P("req"),
        P("req", None),
        P("req"),
    )
    return jax.shard_map(
        functools.partial(local, mesh.shape["req"], mesh.shape["tp"]),
        mesh=mesh,
        in_specs=placed,
        out_specs=P("req", None),
        check_vma=False,
    )
```

time: 93.1 us -> 26.4 us (0.28)
  waiting for transfers between devices: 62.8 us -> 0 us
  Pallas kernels: 0 us -> 17.7 us
  between operations: 13.6 us -> 0.02 us
  other arithmetic: 7.4 us -> 0 us
  matrix products: 6.65 us -> 0 us
  local copies, waits for them, and re-layouts: 2.24 us -> 8.37 us
    all_gather x1 -> x0, waiting for transfers between devices: 38.5 us -> none  [relocate(): collected = lax.all_gather(mixed, 'req', axis=0, tiled=True)]
    psum x1 -> x0, waiting for transfers between devices: 24.2 us -> none  [local(): summed = lax.psum(partial_out, 'tp')]
    pallas_call x0 -> x1, Pallas kernels: none -> 17.7 us  [local(): pl.pallas_call(functools.partial(kernel, n, tp, page), out_shape=jax.Shap...]
    unnamed x8 -> x17, local copies, waits for them, and re-layouts: 0.02 us -> 8.37 us
    dot_general x9 -> x0, matrix products: 6.65 us -> none  [the longest x1 1.71 us: attend(): jnp.einsum('pjc,ptc->pjt', page_query, page_pool[:, :, :head_size], prefe...]
    reduce_sum x4 -> x0, other arithmetic: 3.45 us -> none  [the longest x1 1.21 us: attend(): page_base = jnp.sum(matches.astype(jnp.int32) * offsets, axis=(0, 1))]
    convert_element_type x6 -> x0, other arithmetic: 2.55 us -> none  [the longest x1 1.55 us: local(): mixed = (state.astype(jnp.float32) + summed).astype(jnp.bfloat16)]
    gather x1 -> x0, local copies, waits for them, and re-layouts: 2.02 us -> none  [relocate(): return jnp.take(collected, source_rows, axis=0)]
  transfers between devices with their start and end apart: 2 -> 0, of which waited for: 2 -> 0; matrix products, arithmetic and copies ran while one was open for 0% -> 0% of each run, Pallas kernels for 0% -> 0%
where the time goes in v1:
time: 26.4 us; the launch traced here: 26.1 us
  Pallas kernels  17.7 us (67%)
  local copies, waits for them, and re-layouts  8.37 us (32%)
    pallas_call x1, Pallas kernels, local(): pl.pallas_call(functools.partial(kernel, n, tp, page), out_shape=jax.Shap...  17.7 us
    unnamed x17, local copies, waits for them, and re-layouts  8.37 us

profile of v1, /device:TPU:0, one launch (start us, length us, event | category | flops | bytes accessed | tf_op | source)
XLA Modules:
  0.0 26.1 jit_solution(8637373836249973470)
XLA Ops:
  0.0 0.0 copy-start
  0.0 1.6 %copy-done = bf16[2048,1,512]{2,0,1:T(8,128)(2,1)S(1)} copy-done((bf16[2048,1,512]{2,0,1:T(8,128)(2,1)S(1)}, bf16[2048,1,512]{2,0,1:T(8,128)(2,1)}, u32[]{:S(2)}) %copy-start) | copy-done | bytes 2097176
  1.6 0.0 copy-start.1
  1.6 1.4 %copy-done.1 = bf16[184,1,16,256]{3,2,1,0:T(8,128)(2,1)S(1)} copy-done((bf16[184,1,16,256]{3,2,1,0:T(8,128)(2,1)S(1)}, bf16[184,1,16,256]{3,2,1,0:T(8,128)(2,1)}, u32[]{:S(2)}) %copy-start.1) | copy-done | bytes 1507352
  3.0 0.0 copy-start.2
  3.0 1.2 %copy-done.2 = bf16[1,256,2048]{2,1,0:T(8,128)(2,1)S(1)} copy-done((bf16[1,256,2048]{2,1,0:T(8,128)(2,1)S(1)}, bf16[1,256,2048]{2,1,0:T(8,128)(2,1)}, u32[]{:S(2)}) %copy-start.2) | copy-done | bytes 1048600
  4.2 0.0 copy-start.3
  4.2 0.8 %copy-done.3 = bf16[16,2048]{1,0:T(8,128)(2,1)S(1)} copy-done((bf16[16,2048]{1,0:T(8,128)(2,1)S(1)}, bf16[16,2048]{1,0:T(8,128)(2,1)}, u32[]{:S(2)}) %copy-start.3) | copy-done | bytes 65560
  5.0 0.0 copy-start.4
  5.0 0.7 %copy-done.4 = f32[2048]{0:T(1024)S(1)} copy-done((f32[2048]{0:T(1024)S(1)}, f32[2048]{0:T(1024)}, u32[]{:S(2)}) %copy-start.4) | copy-done | bytes 8216
  5.7 0.0 copy-start.5
  5.7 0.7 %copy-done.5 = s32[16,64]{1,0:T(8,128)S(1)} copy-done((s32[16,64]{1,0:T(8,128)S(1)}, s32[16,64]{1,0:T(8,128)}, u32[]{:S(2)}) %copy-start.5) | copy-done | bytes 4120
  6.4 0.0 copy-start.6
  6.4 0.7 %copy-done.6 = s32[16]{0:T(128)S(1)} copy-done((s32[16]{0:T(128)S(1)}, s32[16]{0:T(128)}, u32[]{:S(2)}) %copy-start.6) | copy-done | bytes 88
  7.1 0.0 copy-start.7
  7.1 0.7 %copy-done.7 = s32[16]{0:T(128)S(1)} copy-done((s32[16]{0:T(128)S(1)}, s32[16]{0:T(128)}, u32[]{:S(2)}) %copy-start.7) | copy-done | bytes 88
  7.7 17.7 %shard_map.82 = bf16[16,2048]{1,0:T(8,128)(2,1)S(1)} custom-call(bf16[16,2048]{1,0:T(8,128)(2,1)S(1)} %copy-done.3, f32[1,2048]{1,0:T(1,128)S(1)} %bitcast.9, bf16[2048,512]{1,0:T(8,128)(2,1)S(1)} %bitcast.6, bf16[256,2048]{1,0:T(8,128)(2,1)S(1)} %bitcast.8, bf16[2944,256]{1,0:T(8,128)(2,1)S(1)} %bitcast.7, s32[1,16]{1,0:T(1,128)S(1)} %bitcast.10, ...), custom_call_target="tpu_custom_call" | custom-call | tf_op jit(solution)/shard_map/pallas_call | solution.py:305
  25.4 0.6 %copy.10 = bf16[16,2048]{1,0:T(8,128)(2,1)} copy(bf16[16,2048]{1,0:T(8,128)(2,1)S(1)} %shard_map.82) | data formatting | bytes 131072
Async XLA Ops:
  0.0 1.6 %copy-start = (bf16[2048,1,512]{2,0,1:T(8,128)(2,1)S(1)}, bf16[2048,1,512]{2,0,1:T(8,128)(2,1)}, u32[]{:S(2)}) copy-start(bf16[2048,1,512]{2,0,1:T(8,128)(2,1)} %param.10) | copy-start | bytes 6291460
  1.6 1.4 %copy-start.1 = (bf16[184,1,16,256]{3,2,1,0:T(8,128)(2,1)S(1)}, bf16[184,1,16,256]{3,2,1,0:T(8,128)(2,1)}, u32[]{:S(2)}) copy-start(bf16[184,1,16,256]{3,2,1,0:T(8,128)(2,1)} %param.12) | copy-start | bytes 4521988
  3.0 1.2 %copy-start.2 = (bf16[1,256,2048]{2,1,0:T(8,128)(2,1)S(1)}, bf16[1,256,2048]{2,1,0:T(8,128)(2,1)}, u32[]{:S(2)}) copy-start(bf16[1,256,2048]{2,1,0:T(8,128)(2,1)} %param.11) | copy-start | bytes 3145732
  4.2 0.8 %copy-start.3 = (bf16[16,2048]{1,0:T(8,128)(2,1)S(1)}, bf16[16,2048]{1,0:T(8,128)(2,1)}, u32[]{:S(2)}) copy-start(bf16[16,2048]{1,0:T(8,128)(2,1)} %state_ref.1) | copy-start | bytes 196612
  5.0 0.7 %copy-start.4 = (f32[2048]{0:T(1024)S(1)}, f32[2048]{0:T(1024)}, u32[]{:S(2)}) copy-start(f32[2048]{0:T(1024)} %param.9) | copy-start | bytes 24580
  5.7 0.7 %copy-start.5 = (s32[16,64]{1,0:T(8,128)S(1)}, s32[16,64]{1,0:T(8,128)}, u32[]{:S(2)}) copy-start(s32[16,64]{1,0:T(8,128)} %table_ref.1) | copy-start | bytes 12292
  6.4 0.7 %copy-start.6 = (s32[16]{0:T(128)S(1)}, s32[16]{0:T(128)}, u32[]{:S(2)}) copy-start(s32[16]{0:T(128)} %param.13) | copy-start | bytes 196
  7.1 0.7 %copy-start.7 = (s32[16]{0:T(128)S(1)}, s32[16]{0:T(128)}, u32[]{:S(2)}) copy-start(s32[16]{0:T(128)} %param.15) | copy-start | bytes 196

commit v2 on v1

--- a/solution.py
+++ b/solution.py
@@ -28,15 +28,20 @@
     n,
     tp,
     page,
-    state_ref,
-    gain_ref,
+    state_hbm,
+    gain_hbm,
     wqkv_hbm,
     wout_hbm,
     pool_hbm,
+    len_hbm,
+    table_hbm,
+    dest_hbm,
+    out_ref,
+    state_ref,
+    gain_ref,
     len_ref,
     table_ref,
     dest_ref,
-    out_ref,
     wqkv,
     wout,
     pool,
@@ -70,7 +75,18 @@
         loads.append(pltpu.make_async_copy(wqkv_hbm.at[span], wqkv.at[span], load_sem.at[step]))
     load_pool = pltpu.make_async_copy(pool_hbm, pool, load_sem.at[steps])
     load_wout = pltpu.make_async_copy(wout_hbm, wout, load_sem.at[steps + 1])
-    for load in loads:
+    small = []
+    for slot, (src, dst) in enumerate(
+        (
+            (state_hbm, state_ref),
+            (gain_hbm, gain_ref),
+            (len_hbm, len_ref),
+            (table_hbm, table_ref),
+            (dest_hbm, dest_ref),
+        )
+    ):
+        small.append(pltpu.make_async_copy(src, dst, load_sem.at[steps + 2 + slot]))
+    for load in small + loads:
         load.start()
     load_pool.start()
     load_wout.start()
@@ -94,6 +110,9 @@
             device_id={"req": me, "tp": lax.rem(my_part + shift, tp)},
             device_id_type=MESH,
         )
+
+    for load in small:
+        load.wait()
 
     wide = state_ref[...].astype(F32)
     factor = lax.rsqrt(jnp.mean(wide * wide, axis=-1, keepdims=True) + 1e-05)
@@ -106,7 +125,8 @@
     freqs = jnp.exp(-math.log(1000000.0) * 2.0 * index / LANES)
     angles = length * freqs
     cosine = jnp.cos(angles)
-    sine = jnp.where(lane < half, -jnp.sin(angles), jnp.sin(angles))
+    sine = jnp.sin(angles)
+    sine = jnp.where(lane < half, -sine, sine)
 
     used = jnp.floor((length + (page - 1)) / page).astype(jnp.int32)
     table = table_ref[...]
@@ -305,9 +325,14 @@
     return pl.pallas_call(
         functools.partial(kernel, n, tp, page),
         out_shape=jax.ShapeDtypeStruct((rows, width), BF16),
-        in_specs=[vmem, vmem, hbm, hbm, hbm, vmem, vmem, vmem],
+        in_specs=[hbm] * 8,
         out_specs=vmem,
         scratch_shapes=[
+            pltpu.VMEM((rows, width), BF16),
+            pltpu.VMEM((1, width), F32),
+            pltpu.VMEM((1, rows), jnp.int32),
+            pltpu.VMEM(page_table.shape, jnp.int32),
+            pltpu.VMEM((1, rows), jnp.int32),
             pltpu.VMEM((width, w_qkv.shape[2]), BF16),
             pltpu.VMEM((w_out.shape[1], width), BF16),
             pltpu.VMEM((tokens, entry), BF16),
@@ -316,7 +341,7 @@
             pltpu.VMEM((n, 2 * blocks, LANES), BF16),
             pltpu.VMEM((n, 2 * blocks, LANES), BF16),
             pltpu.VMEM((tp, rows, chunk), BF16),
-            pltpu.SemaphoreType.DMA((6,)),
+            pltpu.SemaphoreType.DMA((11,)),
             pltpu.SemaphoreType.DMA((tp,)),
             pltpu.SemaphoreType.DMA((tp,)),
             pltpu.SemaphoreType.DMA,
@@ -325,7 +350,7 @@
             pltpu.SemaphoreType.DMA((tp,)),
         ],
         compiler_params=pltpu.CompilerParams(
-            collective_id=0, has_side_effects=True, vmem_limit_bytes=32 * 1024 * 1024
+            collective_id=0, has_side_effects=True, vmem_limit_bytes=60 * 1024 * 1024
         ),
     )(
         state,

time: 26.4 us -> 20 us (0.76)
  local copies, waits for them, and re-layouts: 8.37 us -> 1.47 us
  Pallas kernels: 17.7 us -> 18.4 us
    unnamed x17 -> x1, local copies, waits for them, and re-layouts: 8.37 us -> 1.47 us
    pallas_call x1, Pallas kernels: 17.7 us -> 18.4 us  [local(): pl.pallas_call(functools.partial(kernel, n, tp, page), out_shape=jax.Shap...]
where the time goes in v2:
time: 20 us; the launch traced here: 19.9 us
  Pallas kernels  18.4 us (92%)
  local copies, waits for them, and re-layouts  1.47 us (7%)
    pallas_call x1, Pallas kernels, local(): pl.pallas_call(functools.partial(kernel, n, tp, page), out_shape=jax.Shap...  18.4 us
    unnamed x1, local copies, waits for them, and re-layouts  1.47 us

profile of v2, /device:TPU:0, one launch (start us, length us, event | category | flops | bytes accessed | tf_op | source)
XLA Modules:
  0.0 19.9 jit_solution(1919795259521395689)
XLA Ops:
  0.0 18.4 %shard_map.82 = bf16[16,2048]{1,0:T(8,128)(2,1)} custom-call(bf16[16,2048]{1,0:T(8,128)(2,1)} %state_hbm.1, f32[1,2048]{1,0:T(1,128)} %bitcast.9, bf16[2048,512]{1,0:T(8,128)(2,1)} %bitcast.6, bf16[256,2048]{1,0:T(8,128)(2,1)} %bitcast.8, bf16[2944,256]{1,0:T(8,128)(2,1)} %bitcast.7, s32[1,16]{1,0:T(1,128)} %bitcast.10, s32[16,64]{1,0:T(8,128)} %table_hbm.1, ...), custom_call_target="tpu_custom_call" | custom-call | tf_op jit(solution)/shard_map/pallas_call | solution.py:325
  18.4 1.5 %copy.10 = bf16[16,2048]{1,0:T(8,128)(2,1)} copy(bf16[16,2048]{1,0:T(8,128)(2,1)} %shard_map.82) | data formatting | bytes 131072

commit v3 on v2

--- a/solution.py
+++ b/solution.py
@@ -49,14 +49,11 @@
     arrived,
     outgoing,
     incoming,
-    gathered,
     load_sem,
     part_send,
     part_recv,
     move_send,
     move_recv,
-    gather_send,
-    gather_recv,
 ):
     rows, width = state_ref.shape
     group = wout.shape[0] // LANES
@@ -93,23 +90,15 @@
 
     barrier = pltpu.get_barrier_semaphore()
 
-    def greet(shift, carry):
-        pl.semaphore_signal(
-            barrier,
-            inc=1,
-            device_id={"req": lax.rem(me + shift, n), "tp": my_part},
-            device_id_type=MESH,
-        )
+    def partner(step):
+        other = lax.rem(my_part * n + me + step, n * tp)
+        return {"req": lax.rem(other, n), "tp": other // n}
+
+    def greet(step, carry):
+        pl.semaphore_signal(barrier, inc=1, device_id=partner(step), device_id_type=MESH)
         return carry
 
-    lax.fori_loop(1, n, greet, 0)
-    for shift in range(1, tp):
-        pl.semaphore_signal(
-            barrier,
-            inc=1,
-            device_id={"req": me, "tp": lax.rem(my_part + shift, tp)},
-            device_id_type=MESH,
-        )
+    lax.fori_loop(1, n * tp, greet, 0)
 
     for load in small:
         load.wait()
@@ -229,7 +218,7 @@
     attn = jnp.concatenate([attn[g * rows : (g + 1) * rows] for g in range(group)], axis=1)
 
     load_wout.wait()
-    pl.semaphore_wait(barrier, n - 1 + tp - 1)
+    pl.semaphore_wait(barrier, n * tp - 1)
 
     def columns(part):
         return pl.ds(pl.multiple_of(part * chunk, chunk), chunk)
@@ -246,13 +235,15 @@
 
     for shift in range(1, tp):
         peer = lax.rem(my_part + shift, tp)
-        parts[peer] = jnp.dot(attn, wout[:, columns(peer)], preferred_element_type=F32)
+        parts[peer] = jnp.dot(
+            attn, wout[:, columns(peer)], preferred_element_type=F32
+        ).astype(BF16)
         part_copy(peer, my_part, peer).start()
     summed = jnp.dot(attn, wout[:, columns(my_part)], preferred_element_type=F32)
     for shift in range(1, tp):
         peer = lax.rem(my_part + shift, tp)
         part_copy(peer, peer, peer).wait_recv()
-        summed = summed + arrived[peer]
+        summed = summed + arrived[peer].astype(F32)
     mixed = (state_ref[:, columns(my_part)].astype(F32) + summed).astype(BF16)
 
     stacked = jnp.concatenate(
@@ -261,57 +252,33 @@
     packed = jnp.dot(pack, stacked, preferred_element_type=F32)
     outgoing[...] = packed.reshape(n, 2 * blocks, LANES).astype(BF16)
 
-    def send(shift, carry):
-        peer = lax.rem(me + shift, n)
+    def send(step, carry):
+        place = partner(step)
         pltpu.make_async_remote_copy(
-            src_ref=outgoing.at[peer],
-            dst_ref=incoming.at[me],
+            src_ref=outgoing.at[place["req"]],
+            dst_ref=incoming.at[my_part * n + me],
             send_sem=move_send,
             recv_sem=move_recv,
-            device_id={"req": peer, "tp": my_part},
+            device_id=place,
             device_id_type=MESH,
         ).start()
         return carry
 
-    lax.fori_loop(1, n, send, 0)
-    incoming[me] = outgoing[me]
-    all_but_one = pl.ds(0, n - 1)
-    pltpu.make_async_copy(
-        outgoing.at[all_but_one], incoming.at[all_but_one], move_recv
-    ).wait()
-    received = incoming[...].astype(F32).reshape(total_rows, LANES).astype(BF16)
-    moved = jnp.dot(unpack, received, preferred_element_type=F32).astype(BF16)
-    share = jnp.concatenate(
-        [moved[b * rows : (b + 1) * rows] for b in range(blocks)], axis=1
-    )
-
-    gathered[my_part] = share
-
-    def gather_copy(landing, peer, slot):
-        return pltpu.make_async_remote_copy(
-            src_ref=gathered.at[landing],
-            dst_ref=gathered.at[landing],
-            send_sem=gather_send.at[slot],
-            recv_sem=gather_recv.at[landing],
-            device_id={"req": me, "tp": peer},
-            device_id_type=MESH,
-        )
-
+    lax.fori_loop(1, n * tp, send, 0)
+    incoming[my_part * n + me] = outgoing[me]
+    all_but_one = incoming.at[pl.ds(0, n * tp - 1)]
+    pltpu.make_async_copy(all_but_one, all_but_one, move_recv).wait()
+    for part in range(tp):
+        received = incoming[part * n : (part + 1) * n].astype(F32)
+        received = received.reshape(total_rows, LANES).astype(BF16)
+        moved = jnp.dot(unpack, received, preferred_element_type=F32).astype(BF16)
+        for b in range(blocks):
+            first = part * chunk + b * LANES
+            out_ref[:, first : first + LANES] = moved[b * rows : (b + 1) * rows]
     for shift in range(1, tp):
         peer = lax.rem(my_part + shift, tp)
-        gather_copy(my_part, peer, shift).start()
-    out_ref[:, columns(my_part)] = share
-    for shift in range(1, tp):
-        peer = lax.rem(my_part + shift, tp)
-        gather_copy(peer, peer, shift).wait_recv()
-        out_ref[:, columns(peer)] = gathered[peer]
-    for shift in range(1, tp):
-        peer = lax.rem(my_part + shift, tp)
-        gather_copy(my_part, peer, shift).wait_send()
         part_copy(peer, my_part, peer).wait_send()
-    pltpu.make_async_copy(
-        outgoing.at[all_but_one], incoming.at[all_but_one], move_send
-    ).wait()
+    pltpu.make_async_copy(all_but_one, all_but_one, move_send).wait()
 
 
 def local(n, tp, state, norm_gain, w_qkv, w_out, kv_cache, lengths, page_table, dest_slot):
@@ -324,7 +291,7 @@
     hbm = pl.BlockSpec(memory_space=pltpu.HBM)
     return pl.pallas_call(
         functools.partial(kernel, n, tp, page),
-        out_shape=jax.ShapeDtypeStruct((rows, width), BF16),
+        out_shape=pltpu.VMEM((rows, width), BF16),
         in_specs=[hbm] * 8,
         out_specs=vmem,
         scratch_shapes=[
@@ -336,18 +303,15 @@
             pltpu.VMEM((width, w_qkv.shape[2]), BF16),
             pltpu.VMEM((w_out.shape[1], width), BF16),
             pltpu.VMEM((tokens, entry), BF16),
-            pltpu.VMEM((tp, rows, chunk), F32),
-            pltpu.VMEM((tp, rows, chunk), F32),
+            pltpu.VMEM((tp, rows, chunk), BF16),
+            pltpu.VMEM((tp, rows, chunk), BF16),
             pltpu.VMEM((n, 2 * blocks, LANES), BF16),
-            pltpu.VMEM((n, 2 * blocks, LANES), BF16),
-            pltpu.VMEM((tp, rows, chunk), BF16),
+            pltpu.VMEM((n * tp, 2 * blocks, LANES), BF16),
             pltpu.SemaphoreType.DMA((11,)),
             pltpu.SemaphoreType.DMA((tp,)),
             pltpu.SemaphoreType.DMA((tp,)),
             pltpu.SemaphoreType.DMA,
             pltpu.SemaphoreType.DMA,
-            pltpu.SemaphoreType.DMA((tp,)),
-            pltpu.SemaphoreType.DMA((tp,)),
         ],
         compiler_params=pltpu.CompilerParams(
             collective_id=0, has_side_effects=True, vmem_limit_bytes=60 * 1024 * 1024

time: 20 us -> 16.3 us (0.82)
  Pallas kernels: 18.4 us -> 15.5 us
  local copies, waits for them, and re-layouts: 1.47 us -> 0.63 us
    pallas_call x1, Pallas kernels: 18.4 us -> 15.5 us  [local(): pl.pallas_call(functools.partial(kernel, n, tp, page), out_shape=pltpu.VM...]
    unnamed x1, local copies, waits for them, and re-layouts: 1.47 us -> 0.63 us
where the time goes in v3:
time: 16.3 us; the launch traced here: 16.2 us
  Pallas kernels  15.5 us (95%)
  local copies, waits for them, and re-layouts  0.63 us (4%)
    pallas_call x1, Pallas kernels, local(): pl.pallas_call(functools.partial(kernel, n, tp, page), out_shape=pltpu.VM...  15.5 us
    unnamed x1, local copies, waits for them, and re-layouts  0.63 us

profile of v3, /device:TPU:0, one launch (start us, length us, event | category | flops | bytes accessed | tf_op | source)
XLA Modules:
  0.0 16.2 jit_solution(4480995501990268708)
XLA Ops:
  0.0 15.5 %shard_map.82 = bf16[16,2048]{1,0:T(8,128)(2,1)S(1)} custom-call(bf16[16,2048]{1,0:T(8,128)(2,1)} %state_hbm.1, f32[1,2048]{1,0:T(1,128)} %bitcast.9, bf16[2048,512]{1,0:T(8,128)(2,1)} %bitcast.6, bf16[256,2048]{1,0:T(8,128)(2,1)} %bitcast.8, bf16[2944,256]{1,0:T(8,128)(2,1)} %bitcast.7, s32[1,16]{1,0:T(1,128)} %bitcast.10, s32[16,64]{1,0:T(8,128)} %table_hbm.1, ...), custom_call_target="tpu_custom_call" | custom-call | tf_op jit(solution)/shard_map/pallas_call | solution.py:292
  15.5 0.6 %copy.10 = bf16[16,2048]{1,0:T(8,128)(2,1)} copy(bf16[16,2048]{1,0:T(8,128)(2,1)S(1)} %shard_map.82) | data formatting | bytes 131072

commit v4 on v3

--- a/solution.py
+++ b/solution.py
@@ -45,13 +45,9 @@
     wqkv,
     wout,
     pool,
-    parts,
-    arrived,
     outgoing,
     incoming,
     load_sem,
-    part_send,
-    part_recv,
     move_send,
     move_recv,
 ):
@@ -90,15 +86,31 @@
 
     barrier = pltpu.get_barrier_semaphore()
 
-    def partner(step):
-        other = lax.rem(my_part * n + me + step, n * tp)
-        return {"req": lax.rem(other, n), "tp": other // n}
-
-    def greet(step, carry):
-        pl.semaphore_signal(barrier, inc=1, device_id=partner(step), device_id_type=MESH)
-        return carry
-
-    lax.fori_loop(1, n * tp, greet, 0)
+    def wrapped(value, size):
+        return jnp.where(value >= size, value - size, value)
+
+    def each_partner(act):
+        def visit(shift, carry):
+            peer = wrapped(me + shift, n)
+            for part_shift in range(tp):
+                if part_shift or not isinstance(shift, int) or shift:
+                    act(peer, wrapped(my_part + part_shift, tp))
+            return carry
+
+        if n * tp <= 64:
+            for shift in range(n):
+                visit(shift, 0)
+        else:
+            for part_shift in range(1, tp):
+                act(me, wrapped(my_part + part_shift, tp))
+            lax.fori_loop(1, n, visit, 0)
+
+    def greet(peer, part):
+        pl.semaphore_signal(
+            barrier, inc=1, device_id={"req": peer, "tp": part}, device_id_type=MESH
+        )
+
+    each_partner(greet)
 
     for load in small:
         load.wait()
@@ -218,66 +230,50 @@
     attn = jnp.concatenate([attn[g * rows : (g + 1) * rows] for g in range(group)], axis=1)
 
     load_wout.wait()
+    own_state = (my_part == 0).astype(F32)
+    term = jnp.dot(attn, wout[...], preferred_element_type=F32)
+    mixed = (state_ref[...].astype(F32) * own_state + term).astype(BF16)
+
+    piece_rows = 2 * blocks
+    for part in range(tp):
+        first = part * chunk
+        stacked = jnp.concatenate(
+            [mixed[:, first + b * LANES : first + (b + 1) * LANES] for b in range(blocks)], axis=0
+        )
+        packed = jnp.dot(pack, stacked, preferred_element_type=F32)
+        outgoing[:, part * piece_rows : (part + 1) * piece_rows] = packed.reshape(
+            n, piece_rows, LANES
+        ).astype(BF16)
     pl.semaphore_wait(barrier, n * tp - 1)
-
-    def columns(part):
-        return pl.ds(pl.multiple_of(part * chunk, chunk), chunk)
-
-    def part_copy(slot, landing, peer):
-        return pltpu.make_async_remote_copy(
-            src_ref=parts.at[slot],
-            dst_ref=arrived.at[landing],
-            send_sem=part_send.at[slot],
-            recv_sem=part_recv.at[landing],
-            device_id={"req": me, "tp": peer},
-            device_id_type=MESH,
-        )
-
-    for shift in range(1, tp):
-        peer = lax.rem(my_part + shift, tp)
-        parts[peer] = jnp.dot(
-            attn, wout[:, columns(peer)], preferred_element_type=F32
-        ).astype(BF16)
-        part_copy(peer, my_part, peer).start()
-    summed = jnp.dot(attn, wout[:, columns(my_part)], preferred_element_type=F32)
-    for shift in range(1, tp):
-        peer = lax.rem(my_part + shift, tp)
-        part_copy(peer, peer, peer).wait_recv()
-        summed = summed + arrived[peer].astype(F32)
-    mixed = (state_ref[:, columns(my_part)].astype(F32) + summed).astype(BF16)
-
-    stacked = jnp.concatenate(
-        [mixed[:, b * LANES : (b + 1) * LANES] for b in range(blocks)], axis=0
-    )
-    packed = jnp.dot(pack, stacked, preferred_element_type=F32)
-    outgoing[...] = packed.reshape(n, 2 * blocks, LANES).astype(BF16)
-
-    def send(step, carry):
-        place = partner(step)
+    slot = my_part * n + me
+
+    def send(peer, part):
         pltpu.make_async_remote_copy(
-            src_ref=outgoing.at[place["req"]],
-            dst_ref=incoming.at[my_part * n + me],
+            src_ref=outgoing.at[peer],
+            dst_ref=incoming.at[slot],
             send_sem=move_send,
             recv_sem=move_recv,
-            device_id=place,
+            device_id={"req": peer, "tp": part},
             device_id_type=MESH,
         ).start()
-        return carry
-
-    lax.fori_loop(1, n * tp, send, 0)
-    incoming[my_part * n + me] = outgoing[me]
+
+    each_partner(send)
+    incoming[slot] = outgoing[me]
     all_but_one = incoming.at[pl.ds(0, n * tp - 1)]
     pltpu.make_async_copy(all_but_one, all_but_one, move_recv).wait()
     for part in range(tp):
-        received = incoming[part * n : (part + 1) * n].astype(F32)
-        received = received.reshape(total_rows, LANES).astype(BF16)
-        moved = jnp.dot(unpack, received, preferred_element_type=F32).astype(BF16)
+        moved = None
+        for origin in range(tp):
+            received = incoming[
+                origin * n : (origin + 1) * n, part * piece_rows : (part + 1) * piece_rows
+            ].astype(F32)
+            received = received.reshape(total_rows, LANES).astype(BF16)
+            taken = jnp.dot(unpack, received, preferred_element_type=F32)
+            moved = taken if moved is None else moved + taken
+        moved = moved.astype(BF16)
         for b in range(blocks):
             first = part * chunk + b * LANES
             out_ref[:, first : first + LANES] = moved[b * rows : (b + 1) * rows]
-    for shift in range(1, tp):
-        peer = lax.rem(my_part + shift, tp)
-        part_copy(peer, my_part, peer).wait_send()
     pltpu.make_async_copy(all_but_one, all_but_one, move_send).wait()
 
 
@@ -303,13 +299,9 @@
             pltpu.VMEM((width, w_qkv.shape[2]), BF16),
             pltpu.VMEM((w_out.shape[1], width), BF16),
             pltpu.VMEM((tokens, entry), BF16),
-            pltpu.VMEM((tp, rows, chunk), BF16),
-            pltpu.VMEM((tp, rows, chunk), BF16),
-            pltpu.VMEM((n, 2 * blocks, LANES), BF16),
-            pltpu.VMEM((n * tp, 2 * blocks, LANES), BF16),
+            pltpu.VMEM((n, 2 * blocks * tp, LANES), BF16),
+            pltpu.VMEM((n * tp, 2 * blocks * tp, LANES), BF16),
             pltpu.SemaphoreType.DMA((11,)),
-            pltpu.SemaphoreType.DMA((tp,)),
-            pltpu.SemaphoreType.DMA((tp,)),
             pltpu.SemaphoreType.DMA,
             pltpu.SemaphoreType.DMA,
         ],

time: 16.3 us -> 14.8 us (0.908)
  Pallas kernels: 15.5 us -> 13.9 us
    pallas_call x1, Pallas kernels: 15.5 us -> 13.9 us  [local(): pl.pallas_call(functools.partial(kernel, n, tp, page), out_shape=pltpu.VM...]
where the time goes in v4:
time: 14.8 us; the launch traced here: 14.6 us
  Pallas kernels  13.9 us (94%)
  local copies, waits for them, and re-layouts  0.63 us (4%)
    pallas_call x1, Pallas kernels, local(): pl.pallas_call(functools.partial(kernel, n, tp, page), out_shape=pltpu.VM...  13.9 us
    unnamed x1, local copies, waits for them, and re-layouts  0.63 us

profile of v4, /device:TPU:0, one launch (start us, length us, event | category | flops | bytes accessed | tf_op | source)
XLA Modules:
  0.0 14.6 jit_solution(959973717947502935)
XLA Ops:
  0.0 13.9 %shard_map.82 = bf16[16,2048]{1,0:T(8,128)(2,1)S(1)} custom-call(bf16[16,2048]{1,0:T(8,128)(2,1)} %state_hbm.1, f32[1,2048]{1,0:T(1,128)} %bitcast.9, bf16[2048,512]{1,0:T(8,128)(2,1)} %bitcast.6, bf16[256,2048]{1,0:T(8,128)(2,1)} %bitcast.8, bf16[2944,256]{1,0:T(8,128)(2,1)} %bitcast.7, s32[1,16]{1,0:T(1,128)} %bitcast.10, s32[16,64]{1,0:T(8,128)} %table_hbm.1, ...), custom_call_target="tpu_custom_call" | custom-call | tf_op jit(solution)/shard_map/pallas_call | solution.py:288
  13.9 0.6 %copy.10 = bf16[16,2048]{1,0:T(8,128)(2,1)} copy(bf16[16,2048]{1,0:T(8,128)(2,1)S(1)} %shard_map.82) | data formatting | bytes 131072

commit v5 on v4

--- a/solution.py
+++ b/solution.py
@@ -230,9 +230,8 @@
     attn = jnp.concatenate([attn[g * rows : (g + 1) * rows] for g in range(group)], axis=1)
 
     load_wout.wait()
-    own_state = (my_part == 0).astype(F32)
     term = jnp.dot(attn, wout[...], preferred_element_type=F32)
-    mixed = (state_ref[...].astype(F32) * own_state + term).astype(BF16)
+    mixed = (state_ref[...].astype(F32) * (1.0 / tp) + term).astype(BF16)
 
     piece_rows = 2 * blocks
     for part in range(tp):

time: 14.8 us -> 14.8 us (level)
  no operation moved by 1% of the time
where the time goes in v5:
time: 14.8 us; the launch traced here: 14.6 us
  Pallas kernels  13.9 us (94%)
  local copies, waits for them, and re-layouts  0.63 us (4%)
    pallas_call x1, Pallas kernels, local(): pl.pallas_call(functools.partial(kernel, n, tp, page), out_shape=pltpu.VM...  13.9 us
    unnamed x1, local copies, waits for them, and re-layouts  0.63 us

profile of v5, /device:TPU:0, one launch (start us, length us, event | category | flops | bytes accessed | tf_op | source)
XLA Modules:
  0.0 14.6 jit_solution(13100256670504984592)
XLA Ops:
  0.0 13.9 %shard_map.82 = bf16[16,2048]{1,0:T(8,128)(2,1)S(1)} custom-call(bf16[16,2048]{1,0:T(8,128)(2,1)} %state_hbm.1, f32[1,2048]{1,0:T(1,128)} %bitcast.9, bf16[2048,512]{1,0:T(8,128)(2,1)} %bitcast.6, bf16[256,2048]{1,0:T(8,128)(2,1)} %bitcast.8, bf16[2944,256]{1,0:T(8,128)(2,1)} %bitcast.7, s32[1,16]{1,0:T(1,128)} %bitcast.10, s32[16,64]{1,0:T(8,128)} %table_hbm.1, ...), custom_call_target="tpu_custom_call" | custom-call | tf_op jit(solution)/shard_map/pallas_call | solution.py:287
  13.9 0.6 %copy.10 = bf16[16,2048]{1,0:T(8,128)(2,1)} copy(bf16[16,2048]{1,0:T(8,128)(2,1)S(1)} %shard_map.82) | data formatting | bytes 131072

commit v6 on v3

--- a/solution.py
+++ b/solution.py
@@ -90,15 +90,31 @@
 
     barrier = pltpu.get_barrier_semaphore()
 
-    def partner(step):
-        other = lax.rem(my_part * n + me + step, n * tp)
-        return {"req": lax.rem(other, n), "tp": other // n}
-
-    def greet(step, carry):
-        pl.semaphore_signal(barrier, inc=1, device_id=partner(step), device_id_type=MESH)
-        return carry
-
-    lax.fori_loop(1, n * tp, greet, 0)
+    def wrapped(value, size):
+        return jnp.where(value >= size, value - size, value)
+
+    def each_partner(act):
+        def visit(shift, carry):
+            peer = wrapped(me + shift, n)
+            for part_shift in range(tp):
+                if part_shift or not isinstance(shift, int) or shift:
+                    act(peer, wrapped(my_part + part_shift, tp))
+            return carry
+
+        if n * tp <= 64:
+            for shift in range(n):
+                visit(shift, 0)
+        else:
+            for part_shift in range(1, tp):
+                act(me, wrapped(my_part + part_shift, tp))
+            lax.fori_loop(1, n, visit, 0)
+
+    def greet(peer, part):
+        pl.semaphore_signal(
+            barrier, inc=1, device_id={"req": peer, "tp": part}, device_id_type=MESH
+        )
+
+    each_partner(greet)
 
     for load in small:
         load.wait()
@@ -252,20 +268,20 @@
     packed = jnp.dot(pack, stacked, preferred_element_type=F32)
     outgoing[...] = packed.reshape(n, 2 * blocks, LANES).astype(BF16)
 
-    def send(step, carry):
-        place = partner(step)
+    slot = my_part * n + me
+
+    def send(peer, part):
         pltpu.make_async_remote_copy(
-            src_ref=outgoing.at[place["req"]],
-            dst_ref=incoming.at[my_part * n + me],
+            src_ref=outgoing.at[peer],
+            dst_ref=incoming.at[slot],
             send_sem=move_send,
             recv_sem=move_recv,
-            device_id=place,
+            device_id={"req": peer, "tp": part},
             device_id_type=MESH,
         ).start()
-        return carry
-
-    lax.fori_loop(1, n * tp, send, 0)
-    incoming[my_part * n + me] = outgoing[me]
+
+    each_partner(send)
+    incoming[slot] = outgoing[me]
     all_but_one = incoming.at[pl.ds(0, n * tp - 1)]
     pltpu.make_async_copy(all_but_one, all_but_one, move_recv).wait()
     for part in range(tp):

time: 16.3 us -> 15.8 us (0.969)
  Pallas kernels: 15.5 us -> 15 us
    pallas_call x1, Pallas kernels: 15.5 us -> 15 us  [local(): pl.pallas_call(functools.partial(kernel, n, tp, page), out_shape=pltpu.VM...]
where the time goes in v6:
time: 15.8 us; the launch traced here: 15.6 us
  Pallas kernels  15 us (95%)
  local copies, waits for them, and re-layouts  0.63 us (4%)
    pallas_call x1, Pallas kernels, local(): pl.pallas_call(functools.partial(kernel, n, tp, page), out_shape=pltpu.VM...  15 us
    unnamed x1, local copies, waits for them, and re-layouts  0.63 us

profile of v6, /device:TPU:0, one launch (start us, length us, event | category | flops | bytes accessed | tf_op | source)
XLA Modules:
  0.0 15.6 jit_solution(9496854823731440699)
XLA Ops:
  0.0 15.0 %shard_map.82 = bf16[16,2048]{1,0:T(8,128)(2,1)S(1)} custom-call(bf16[16,2048]{1,0:T(8,128)(2,1)} %state_hbm.1, f32[1,2048]{1,0:T(1,128)} %bitcast.9, bf16[2048,512]{1,0:T(8,128)(2,1)} %bitcast.6, bf16[256,2048]{1,0:T(8,128)(2,1)} %bitcast.8, bf16[2944,256]{1,0:T(8,128)(2,1)} %bitcast.7, s32[1,16]{1,0:T(1,128)} %bitcast.10, s32[16,64]{1,0:T(8,128)} %table_hbm.1, ...), custom_call_target="tpu_custom_call" | custom-call | tf_op jit(solution)/shard_map/pallas_call | solution.py:308
  15.0 0.6 %copy.10 = bf16[16,2048]{1,0:T(8,128)(2,1)} copy(bf16[16,2048]{1,0:T(8,128)(2,1)S(1)} %shard_map.82) | data formatting | bytes 131072
